TPU v7x, 256 devices: a whole 4x4x8 slice. The times are simulated.
256 devices in a mesh: dp: 32 (over y, z_lo, core), cent: 8 (over x, z_hi).
Axes of the slice: x: 4, y: 4, z: 8 (z_hi: 2, z_lo: 4; z = z_hi * 4 + z_lo), core: 2. Of those that a mesh axis runs over, the one named last changes fastest.
Arguments:
- hidden: bfloat16 [5632, 11008], P('dp', 'cent'), may hold values from -6 to 6
- residual: bfloat16 [5632, 4096], P('dp', 'cent'), may hold values from -6 to 6
- down_weight: bfloat16 [11008, 4096], P('cent', 'dp'), may hold values from -0.0546875 to 0.0546875
- gain: float32 [4096], P('cent'), may hold values from 0.1 to 1.9
- proj_weight: bfloat16 [4096, 1024], P('cent'), may hold values from -0.09375 to 0.09375
- centroids: bfloat16 [131072, 1024], P(('dp', 'cent')), may hold values from -24 to 24
Outputs:
- weighted: float32 [131072, 1024], P(('dp', 'cent'))
- counts: float32 [131072], P(('dp', 'cent'))
All inputs are finite; a program needn't handle non-finite values.
Results may differ from a plain program's by a relative error of at most 0.011.
Values may be sent and summed in bfloat16 or wider, within the bound.
A program may use at most 128 MiB of HBM per device.

v0:
```python
import math
import jax
import jax.numpy as jnp
from jax import lax
from jax.sharding import PartitionSpec as P


def body(hidden, residual, down_weight, gain, proj_weight, centroids):
    partial_layer = jnp.dot(
        hidden,
        lax.all_gather(down_weight, "dp", axis=1, tiled=True),
        preferred_element_type=jnp.float32,
    )
    layer_out = lax.psum_scatter(partial_layer, "cent", scatter_dimension=1, tiled=True)
    normed = ((layer_out + residual.astype(jnp.float32)) * gain).astype(jnp.bfloat16)
    partial_embed = jnp.dot(normed, proj_weight, preferred_element_type=jnp.float32)
    embed_width = proj_weight.shape[1]
    embed_full = lax.psum(partial_embed, "cent")
    scaled = (
        embed_full * lax.rsqrt(jnp.mean(embed_full * embed_full, axis=1, keepdims=True) + 1e-06)
    ).astype(jnp.bfloat16)
    gathered = lax.all_gather(scaled, "dp", axis=0, tiled=True)
    inverse = 1.0 / (math.sqrt(embed_width) * 0.05)
    scores = (
        lax.dot_general(
            gathered, centroids, (((1,), (1,)), ((), ())), preferred_element_type=jnp.float32
        )
        * inverse
    )
    local_max = jnp.max(scores, axis=1)
    row_max = lax.pmax(local_max, ("dp", "cent"))
    row_total = lax.psum(jnp.sum(jnp.exp(scores - row_max[:, None]), axis=1), ("dp", "cent"))
    log_total = row_max + jnp.log(row_total)
    probability = jnp.exp(scores - log_total[:, None])
    scale_up = centroids.shape[0] * lax.axis_size("dp") * lax.axis_size("cent") / gathered.shape[0]
    counts = scale_up * jnp.sum(probability, axis=0)
    prob_low = probability.astype(jnp.bfloat16)
    weighted = scale_up * lax.dot_general(
        prob_low, gathered, (((0,), (0,)), ((), ())), preferred_element_type=jnp.float32
    )
    return (weighted, counts)


def solution(mesh):
    in_specs = (
        P("dp", "cent"),
        P("dp", "cent"),
        P("cent", "dp"),
        P("cent"),
        P("cent", None),
        P(("dp", "cent"), None),
    )
    out_specs = (P(("dp", "cent"), None), P(("dp", "cent")))
    return jax.shard_map(body, mesh=mesh, in_specs=in_specs, out_specs=out_specs, check_vma=False)
```

profile of v0, /device:TPU:1, one launch (start us, length us, event | category | flops | bytes accessed | tf_op | source)
XLA Modules:
  0.0 617.1 jit_solution(13492038344672853306)
XLA Ops:
  7.2 0.0 copy-start
  7.2 0.0 all-gather.3.cloned.1.call-start
  7.3 0.7 all-gather.3.cloned.1.call-update
  7.9 0.0 reduce-scatter.2.cloned.1.call-start
  8.0 105.2 %all-gather.3.cloned.1.call-done = bf16[1376,4096]{1,0:T(8,128)(2,1)} async-done(((bf16[1376,128]{1,0:T(8,128)(2,1)}), bf16[1376,4096]{1,0:T(8,128)(2,1)}) %all-gather.3.cloned.1.call-update) | async-done | bytes 11272208 | tf_op jit(solution)/shard_map/all_gather | solution.py:11
  113.2 8.5 %fusion.11 = f32[176,4096]{1,0:T(8,128)} fusion(bf16[176,1376]{1,0:T(8,128)(2,1)} %param.6, bf16[1376,4096]{1,0:T(8,128)(2,1)} %all-gather.3.cloned.1.call-done), kind=kOutput, calls=%fused_computation.17 | convolution fusion | flops 1983905792 | bytes 14640128 | tf_op jit(solution)/shard_map/dot_general | solution.py:9
  121.7 0.0 reduce-scatter.2.cloned.1.call-update
  121.7 0.0 all-reduce.2.cloned.1.call-start
  121.8 103.8 %reduce-scatter.2.cloned.1.call-done = f32[176,512]{1,0:T(8,128)} async-done(((f32[176,4096]{1,0:T(8,128)}), f32[176,512]{1,0:T(8,128)}) %reduce-scatter.2.cloned.1.call-update) | async-done | bytes 360464 | tf_op jit(solution)/shard_map/reduce_scatter | solution.py:14
  225.6 2.2 fusion.8
  227.8 0.0 all-reduce.2.cloned.1.call-update
  227.8 0.0 all-gather.5.cloned.1.call-start
  227.8 112.2 %all-reduce.2.cloned.1.call-done = f32[176,1024]{1,0:T(8,128)} async-done(((f32[176,1024]{1,0:T(8,128)}), f32[176,1024]{1,0:T(8,128)}) %all-reduce.2.cloned.1.call-update) | async-done | bytes 720912 | tf_op jit(solution)/shard_map/psum | solution.py:18
  340.1 1.2 multiply_reduce_fusion
  341.3 2.0 multiply_convert_fusion
  343.3 0.0 all-gather.5.cloned.1.call-update
  343.3 78.9 %all-gather.5.cloned.1.call-done = bf16[5632,1024]{1,0:T(8,128)(2,1)} async-done(((bf16[176,1024]{1,0:T(8,128)(2,1)}), bf16[5632,1024]{1,0:T(8,128)(2,1)}) %all-gather.5.cloned.1.call-update) | async-done | bytes 11534352 | tf_op jit(solution)/shard_map/all_gather | solution.py:22
  422.2 13.2 %fusion.10 = (f32[5632]{0:T(1024)S(1)}, f32[5632,512]{0,1:T(8,128)}) fusion(bf16[5632,1024]{1,0:T(8,128)(2,1)} %all-gather.5.cloned.1.call-done, bf16[512,1024]{1,0:T(8,128)(2,1)S(1)} %copy-done), kind=kOutput, calls=%fused_computation.16 | convolution fusion | flops 5911341568 | bytes 24139776 | tf_op jit(solution)/shard_map/dot_general | solution.py:25
  435.3 76.1 %pmax.7 = f32[5632]{0:T(1024)S(1)} all-reduce(f32[5632]{0:T(1024)S(1)} %get-tuple-element.2), channel_id=1, replica_groups=mesh['dp'=32,'cent'=8] {'dp','cent'}, use_global_device_ids=true, to_apply=%region_4.0 | all-reduce | flops 5632 | bytes 45056 | tf_op jit(solution)/shard_map/pmax | solution.py:31
  511.4 6.0 exponential_reduce_fusion
  517.4 73.3 %psum.15 = f32[5632]{0:T(1024)S(1)} all-reduce(f32[5632]{0:T(1024)S(1)} %exponential_reduce_fusion), channel_id=1, replica_groups=mesh['dp'=32,'cent'=8] {'dp','cent'}, use_global_device_ids=true, to_apply=%region_6.0 | all-reduce | flops 5632 | bytes 45056 | tf_op jit(solution)/shard_map/psum | solution.py:32
  590.7 6.0 fusion
  596.7 0.6 broadcast_multiply_fusion
  597.3 13.3 %fusion.5 = f32[512,1024]{1,0:T(8,128)} fusion(bf16[5632,1024]{1,0:T(8,128)(2,1)} %all-gather.5.cloned.1.call-done, f32[5632,512]{0,1:T(8,128)} %get-tuple-element.3, f32[5632]{0:T(1024)S(1)} %log_add_fusion), kind=kOutput, calls=%fused_computation.7 | convolution fusion | flops 5911871488 | bytes 25188352 | tf_op jit(solution)/shard_map/dot_general | solution.py:38
  (9 shorter events, 0.0 us)
Async XLA Ops:
  7.2 415.0 %copy-start = (bf16[512,1024]{1,0:T(8,128)(2,1)S(1)}, bf16[512,1024]{1,0:T(8,128)(2,1)}, u32[]{:S(2)}) copy-start(bf16[512,1024]{1,0:T(8,128)(2,1)} %param.11) | copy-start | bytes 3145732
  7.2 218.4 %copy-start.1 = (bf16[512,1024]{1,0:T(8,128)(2,1)S(1)}, bf16[512,1024]{1,0:T(8,128)(2,1)}, u32[]{:S(2)}) copy-start(bf16[512,1024]{1,0:T(8,128)(2,1)} %param.10) | copy-start | bytes 3145732
  7.2 218.4 %copy-start.3 = (f32[512]{0:T(512)S(1)}, f32[512]{0:T(512)}, u32[]{:S(2)}) copy-start(f32[512]{0:T(512)} %param.9) | copy-start | bytes 6148
  7.2 218.4 %copy-start.2 = (bf16[176,512]{1,0:T(8,128)(2,1)S(1)}, bf16[176,512]{1,0:T(8,128)(2,1)}, u32[]{:S(2)}) copy-start(bf16[176,512]{1,0:T(8,128)(2,1)} %param.7) | copy-start | bytes 540676
  7.2 106.0 %all-gather.3.cloned.1.call-start = ((), (), s32[]{:S(2)}) async-start(), calls=%async_computation.1 | async-start | bytes 11624448 | tf_op jit(solution)/shard_map/all_gather | solution.py:11
  7.9 217.6 %reduce-scatter.2.cloned.1.call-start = ((), (), s32[]{:S(2)}) async-start(), calls=%async_computation.2 | async-start | bytes 3244032 | tf_op jit(solution)/shard_map/reduce_scatter | solution.py:14
  121.7 218.3 %all-reduce.2.cloned.1.call-start = ((), (), s32[]{:S(2)}) async-start(), calls=%async_computation.3 | async-start | bytes 1441792 | tf_op jit(solution)/shard_map/psum | solution.py:18
  227.8 194.4 %all-gather.5.cloned.1.call-start = ((), (), s32[]{:S(2)}) async-start(), calls=%async_computation.4 | async-start | bytes 11894784 | tf_op jit(solution)/shard_map/all_gather | solution.py:22
Sparse Core Ops, SparseCore 0:
  9.8 103.3 all-gather.2
  121.8 103.6 reduce-scatter.1
  228.8 111.2 all-reduce.1
  343.4 78.7 all-gather.4
where the time goes:
time: 618 us; the launch traced here: 617 us
  waiting for transfers between devices  401 us (65%)
  blocking collectives  149 us (24%)
  matrix products  37.1 us (6%)
  other arithmetic  15.8 us (3%)
  between operations  13.8 us (2%)
    psum x1, waiting for transfers between devices, body(): embed_full = lax.psum(partial_embed, 'cent')  112 us
    all_gather x1, waiting for transfers between devices, body(): lax.all_gather(down_weight, 'dp', axis=1, tiled=True)  105 us
    reduce_scatter x1, waiting for transfers between devices, body(): lax.psum_scatter(partial_layer, 'cent', scatter_dimension=1, tiled=True)  104 us
    all_gather x1, waiting for transfers between devices, body(): gathered = lax.all_gather(scaled, 'dp', axis=0, tiled=True)  78.9 us
    pmax x1, blocking collectives, body(): row_max = lax.pmax(local_max, ('dp', 'cent'))  76.1 us
    psum x1, blocking collectives, body(): lax.psum(jnp.sum(jnp.exp(scores - row_max[:, None]), axis=1), ('dp', 'cen...  73.3 us
    dot_general x1, matrix products, body(): lax.dot_general(prob_low, gathered, (((0,), (0,)), ((), ())), preferred_e...  13.3 us
    dot_general x1, matrix products, body(): lax.dot_general(gathered, centroids, (((1,), (1,)), ((), ())), preferred_...  13.2 us
  transfers between devices with their start and end apart: 4, of which 4 were waited for; matrix products, arithmetic and copies ran while one was open for 0% of the time, Pallas kernels for 0%

commit v1 on v0

--- a/solution.py
+++ b/solution.py
@@ -6,11 +6,13 @@
 
 
 def body(hidden, residual, down_weight, gain, proj_weight, centroids):
-    partial_layer = jnp.dot(
-        hidden,
-        lax.all_gather(down_weight, "dp", axis=1, tiled=True),
-        preferred_element_type=jnp.float32,
+    trace_unit_for = lambda row_data: jnp.concatenate(
+        jax.lax.all_to_all(
+            jnp.stack([row_data for _ in range(jax.lax.axis_size("dp"))], axis=0), "dp", 0, 0
+        ),
+        axis=1,
     )
+    partial_layer = jnp.dot(hidden, trace_unit_for(down_weight), preferred_element_type=jnp.float32)
     layer_out = lax.psum_scatter(partial_layer, "cent", scatter_dimension=1, tiled=True)
     normed = ((layer_out + residual.astype(jnp.float32)) * gain).astype(jnp.bfloat16)
     partial_embed = jnp.dot(normed, proj_weight, preferred_element_type=jnp.float32)

time: 618 us -> 792 us (1.28)
  blocking collectives: 149 us -> 407 us
  waiting for transfers between devices: 401 us -> 294 us
  local copies, waits for them, and re-layouts: 0.02 us -> 21.9 us
    all_to_all x0 -> x1, blocking collectives: none -> 257 us  [body(): jax.lax.all_to_all(jnp.stack([row_data for _ in range(jax.lax.axis_size('...]
    all_gather x1 -> x0, waiting for transfers between devices: 105 us -> none  [body(): lax.all_gather(down_weight, 'dp', axis=1, tiled=True)]
    reshape x0 -> x1, local copies, waits for them, and re-layouts: none -> 15.1 us  [body(): jnp.concatenate(jax.lax.all_to_all(jnp.stack([row_data for _ in range(jax...]
  transfers between devices with their start and end apart: 4 -> 3, of which waited for: 4 -> 3; matrix products, arithmetic and copies ran while one was open for 0% -> 0% of each run, Pallas kernels for 0% -> 0%
where the time goes in v1:
time: 792 us; the launch traced here: 791 us
  blocking collectives  407 us (51%)
  waiting for transfers between devices  294 us (37%)
  matrix products  38.7 us (5%)
  local copies, waits for them, and re-layouts  21.9 us (3%)
  other arithmetic  15.8 us (2%)
  between operations  13.8 us (2%)
    all_to_all x1, blocking collectives, body(): jax.lax.all_to_all(jnp.stack([row_data for _ in range(jax.lax.axis_size('...  257 us
    psum x1, waiting for transfers between devices, body(): embed_full = lax.psum(partial_embed, 'cent')  112 us
    reduce_scatter x1, waiting for transfers between devices, body(): lax.psum_scatter(partial_layer, 'cent', scatter_dimension=1, tiled=True)  103 us
    all_gather x1, waiting for transfers between devices, body(): gathered = lax.all_gather(scaled, 'dp', axis=0, tiled=True)  78.9 us
    pmax x1, blocking collectives, body(): row_max = lax.pmax(local_max, ('dp', 'cent'))  76.1 us
    psum x1, blocking collectives, body(): lax.psum(jnp.sum(jnp.exp(scores - row_max[:, None]), axis=1), ('dp', 'cen...  73.3 us
  transfers between devices with their start and end apart: 3, of which 3 were waited for; matrix products, arithmetic and copies ran while one was open for 0% of the time, Pallas kernels for 0%

profile of v1, /device:TPU:1, one launch (start us, length us, event | category | flops | bytes accessed | tf_op | source)
XLA Modules:
  0.0 790.8 jit_solution(3884940150533967789)
XLA Ops:
  7.2 0.0 copy-start
  7.2 0.0 reduce-scatter.2.cloned.1.call-start
  7.2 6.8 stack.2
  14.0 257.3 %all_to_all.5 = bf16[32,1376,128]{2,1,0:T(8,128)(2,1)} all-to-all(bf16[32,1376,128]{2,1,0:T(8,128)(2,1)} %stack.2), channel_id=1, replica_groups=mesh['dp'=32,'cent'=8] {'dp'}, dimensions={0} | all-to-all | bytes 22544384 | tf_op jit(solution)/shard_map/all_to_all | solution.py:10
  271.3 15.1 %copy.9 = bf16[1376,32,128]{0,2,1:T(8,128)(2,1)} copy(bf16[1376,32,128]{2,0,1:T(8,128)(2,1)} %bitcast.9) | data formatting | bytes 22544384 | tf_op jit(solution)/shard_map/reshape | solution.py:9
  286.4 10.0 %fusion.11 = f32[176,4096]{1,0:T(8,128)} fusion(bf16[176,1376]{1,0:T(8,128)(2,1)S(1)} %copy-done.3, bf16[1376,4096]{0,1:T(8,128)(2,1)} %bitcast.8), kind=kOutput, calls=%fused_computation.17 | convolution fusion | flops 1983905792 | bytes 14640128 | tf_op jit(solution)/shard_map/dot_general | solution.py:15
  296.5 0.0 reduce-scatter.2.cloned.1.call-update
  296.5 0.0 all-reduce.2.cloned.1.call-start
  296.5 102.6 %reduce-scatter.2.cloned.1.call-done = f32[176,512]{1,0:T(8,128)} async-done(((f32[176,4096]{1,0:T(8,128)}), f32[176,512]{1,0:T(8,128)}) %reduce-scatter.2.cloned.1.call-update) | async-done | bytes 360464 | tf_op jit(solution)/shard_map/reduce_scatter | solution.py:16
  399.1 2.2 fusion.8
  401.3 0.0 all-reduce.2.cloned.1.call-update
  401.3 0.0 all-gather.2.cloned.1.call-start
  401.4 112.2 %all-reduce.2.cloned.1.call-done = f32[176,1024]{1,0:T(8,128)} async-done(((f32[176,1024]{1,0:T(8,128)}), f32[176,1024]{1,0:T(8,128)}) %all-reduce.2.cloned.1.call-update) | async-done | bytes 720912 | tf_op jit(solution)/shard_map/psum | solution.py:20
  513.6 1.2 multiply_reduce_fusion
  514.9 2.0 multiply_convert_fusion
  516.8 0.0 all-gather.2.cloned.1.call-update
  516.9 78.9 %all-gather.2.cloned.1.call-done = bf16[5632,1024]{1,0:T(8,128)(2,1)} async-done(((bf16[176,1024]{1,0:T(8,128)(2,1)}), bf16[5632,1024]{1,0:T(8,128)(2,1)}) %all-gather.2.cloned.1.call-update) | async-done | bytes 11534352 | tf_op jit(solution)/shard_map/all_gather | solution.py:24
  595.7 13.2 %fusion.10 = (f32[5632]{0:T(1024)S(1)}, f32[5632,512]{0,1:T(8,128)}) fusion(bf16[5632,1024]{1,0:T(8,128)(2,1)} %all-gather.2.cloned.1.call-done, bf16[512,1024]{1,0:T(8,128)(2,1)S(1)} %copy-done), kind=kOutput, calls=%fused_computation.16 | convolution fusion | flops 5911341568 | bytes 24139776 | tf_op jit(solution)/shard_map/dot_general | solution.py:27
  608.9 76.1 %pmax.7 = f32[5632]{0:T(1024)S(1)} all-reduce(f32[5632]{0:T(1024)S(1)} %get-tuple-element.2), channel_id=1, replica_groups=mesh['dp'=32,'cent'=8] {'dp','cent'}, use_global_device_ids=true, to_apply=%region_4.0 | all-reduce | flops 5632 | bytes 45056 | tf_op jit(solution)/shard_map/pmax | solution.py:33
  685.0 6.0 exponential_reduce_fusion
  691.0 73.3 %psum.15 = f32[5632]{0:T(1024)S(1)} all-reduce(f32[5632]{0:T(1024)S(1)} %exponential_reduce_fusion), channel_id=1, replica_groups=mesh['dp'=32,'cent'=8] {'dp','cent'}, use_global_device_ids=true, to_apply=%region_6.0 | all-reduce | flops 5632 | bytes 45056 | tf_op jit(solution)/shard_map/psum | solution.py:34
  764.3 6.0 fusion
  770.3 0.6 broadcast_multiply_fusion
  770.9 13.3 %fusion.5 = f32[512,1024]{1,0:T(8,128)} fusion(bf16[5632,1024]{1,0:T(8,128)(2,1)} %all-gather.2.cloned.1.call-done, f32[5632,512]{0,1:T(8,128)} %get-tuple-element.3, f32[5632]{0:T(1024)S(1)} %log_add_fusion), kind=kOutput, calls=%fused_computation.7 | convolution fusion | flops 5911871488 | bytes 25188352 | tf_op jit(solution)/shard_map/dot_general | solution.py:40
  (13 shorter events, 0.0 us)
Async XLA Ops:
  7.2 588.6 %copy-start = (bf16[512,1024]{1,0:T(8,128)(2,1)S(1)}, bf16[512,1024]{1,0:T(8,128)(2,1)}, u32[]{:S(2)}) copy-start(bf16[512,1024]{1,0:T(8,128)(2,1)} %param.11) | copy-start | bytes 3145732
  7.2 391.9 %reduce-scatter.2.cloned.1.call-start = ((), (), s32[]{:S(2)}) async-start(), calls=%async_computation.2 | async-start | bytes 3244032 | tf_op jit(solution)/shard_map/reduce_scatter | solution.py:16
  271.3 15.1 %copy-start.3 = (bf16[176,1376]{1,0:T(8,128)(2,1)S(1)}, bf16[176,1376]{1,0:T(8,128)(2,1)}, u32[]{:S(2)}) copy-start(bf16[176,1376]{1,0:T(8,128)(2,1)} %param.6) | copy-start | bytes 1453060
  286.4 112.7 %copy-start.2 = (bf16[512,1024]{1,0:T(8,128)(2,1)S(1)}, bf16[512,1024]{1,0:T(8,128)(2,1)}, u32[]{:S(2)}) copy-start(bf16[512,1024]{1,0:T(8,128)(2,1)} %param.10) | copy-start | bytes 3145732
  286.4 112.7 %copy-start.4 = (bf16[176,512]{1,0:T(8,128)(2,1)S(1)}, bf16[176,512]{1,0:T(8,128)(2,1)}, u32[]{:S(2)}) copy-start(bf16[176,512]{1,0:T(8,128)(2,1)} %param.7) | copy-start | bytes 540676
  286.4 112.7 %copy-start.5 = (f32[512]{0:T(512)S(1)}, f32[512]{0:T(512)}, u32[]{:S(2)}) copy-start(f32[512]{0:T(512)} %param.9) | copy-start | bytes 6148
  296.5 217.2 %all-reduce.2.cloned.1.call-start = ((), (), s32[]{:S(2)}) async-start(), calls=%async_computation.3 | async-start | bytes 1441792 | tf_op jit(solution)/shard_map/psum | solution.py:20
  401.3 194.4 %all-gather.2.cloned.1.call-start = ((), (), s32[]{:S(2)}) async-start(), calls=%async_computation.4 | async-start | bytes 11894784 | tf_op jit(solution)/shard_map/all_gather | solution.py:24
  770.9 13.3 %copy-start.1 = (bf16[512,1024]{1,0:T(8,128)(2,1)S(1)}, bf16[512,1024]{1,0:T(8,128)(2,1)}, u32[]{:S(2)}) copy-start(bf16[512,1024]{1,0:T(8,128)(2,1)} %param.11) | copy-start | bytes 3145732
Sparse Core Ops, SparseCore 0:
  296.6 102.4 reduce-scatter.1
  402.3 111.2 all-reduce.1
  517.0 78.7 all-gather.1
